TPU v7x, 32 devices: a whole 2x2x4 slice. The times are simulated.
32 devices in a mesh: fsdp: 8 (over y, x, core), sp: 4 (over z).
Axes of the slice: x: 2, y: 2, z: 4, core: 2. Of those that a mesh axis runs over, the one named last changes fastest.
Arguments:
- hidden_in: bfloat16 [8, 1024, 2048], P('fsdp', 'sp'), may hold values from -6 to 6
- segments: int32 [8, 1024], P('fsdp'), may hold values from 0 to 3, never falling along the last dimension, each value on 1 to 640 neighbouring positions
- ln1_gain: float32 [2048], replicated, may hold values from 0.5 to 1.5
- ln1_bias: float32 [2048], replicated, may hold values from -1 to 1
- ln2_gain: float32 [2048], replicated, may hold values from 0.5 to 1.5
- ln2_bias: float32 [2048], replicated, may hold values from -1 to 1
- w_qkv: bfloat16 [6144, 2048], P('fsdp'), may hold values from -0.125 to 0.125
- b_qkv: float32 [6144], replicated, may hold values from -1 to 1
- w_dense: bfloat16 [2048, 2048], P('fsdp'), may hold values from -0.75 to 0.75
- b_dense: float32 [2048], replicated, may hold values from -1 to 1
- w_up: bfloat16 [8192, 2048], P('fsdp'), may hold values from -0.125 to 0.125
- b_up: float32 [8192], replicated, may hold values from -1 to 1
- w_down: bfloat16 [8192, 2048], P('fsdp'), may hold values from -0.0625 to 0.0625
- b_down: float32 [2048], replicated, may hold values from -1 to 1
- cotangent: bfloat16 [8, 1024, 2048], P('fsdp', 'sp'), may hold values from -6 to 6
Outputs:
- output: bfloat16 [8, 1024, 2048], P('fsdp', 'sp')
- input_grad: bfloat16 [8, 1024, 2048], P('fsdp', 'sp')
- grad_ln1_gain: float32 [2048], P('fsdp')
- grad_ln1_bias: float32 [2048], P('fsdp')
- grad_ln2_gain: float32 [2048], P('fsdp')
- grad_ln2_bias: float32 [2048], P('fsdp')
- grad_w_qkv: float32 [6144, 2048], P('fsdp')
- grad_b_qkv: float32 [6144], P('fsdp')
- grad_w_dense: float32 [2048, 2048], P('fsdp')
- grad_b_dense: float32 [2048], P('fsdp')
- grad_w_up: float32 [8192, 2048], P('fsdp')
- grad_b_up: float32 [8192], P('fsdp')
- grad_w_down: float32 [8192, 2048], P('fsdp')
- grad_b_down: float32 [2048], P('fsdp')
Inputs may be any that keep to these rules, and one draw needn't show every extreme that they name: `segments`: along each sequence the segment numbers never fall; each document is one run of 1 to 640 positions, and some document has exactly 640.
All inputs are finite; a program needn't handle non-finite values.
Results may differ from a plain program's by a relative error of at most 0.011.
Values may be sent and summed in bfloat16 or wider, within the bound.
A program may use at most 704 MiB of HBM per device.

v0:
```python
import math
import jax
import jax.numpy as jnp
from jax import lax
from jax.sharding import PartitionSpec as P

HEADS = 8
HEAD_DIM = 256
ROT = 64
EPSILON = 1e-05
NEGATIVE = -1e30
ROOT_HALF = 0.7071067811865476
ROOT_TWO_PI = 2.5066282746310002


def contract_rows(former, latter):
    return lax.dot_general(
        former, latter, (((0,), (0,)), ((), ())), preferred_element_type=jnp.float32
    )


def times_transposed(former, latter):
    return lax.dot_general(
        former, latter, (((1,), (1,)), ((), ())), preferred_element_type=jnp.float32
    )


def norm_forward(inputs, norm_gain, norm_shift):
    average = jnp.mean(inputs, axis=-1, keepdims=True)
    centred = inputs - average
    variance = jnp.mean(centred * centred, axis=-1, keepdims=True)
    inverse = lax.rsqrt(variance + EPSILON)
    scaled = centred * inverse
    return (scaled * norm_gain + norm_shift, scaled, inverse)


def norm_backward(upstream, scaled, inverse, norm_gain):
    weighted = upstream * norm_gain
    first_mean = jnp.mean(weighted, axis=-1, keepdims=True)
    second_mean = jnp.mean(weighted * scaled, axis=-1, keepdims=True)
    input_part = inverse * (weighted - first_mean - scaled * second_mean)
    return (input_part, jnp.sum(upstream * scaled, axis=0), jnp.sum(upstream, axis=0))


def gelu_pair(hidden):
    cumulative = 0.5 * (1.0 + jax.scipy.special.erf(hidden * ROOT_HALF))
    return (
        hidden * cumulative,
        cumulative + hidden * jnp.exp(-0.5 * hidden * hidden) / ROOT_TWO_PI,
    )


def rotary_tables(segment_rows):
    length = segment_rows.shape[-1]
    places = jnp.arange(length, dtype=jnp.int32)
    changes = jnp.concatenate(
        [
            jnp.ones_like(segment_rows[..., :1]),
            (segment_rows[..., 1:] != segment_rows[..., :-1]).astype(jnp.int32),
        ],
        axis=-1,
    )
    first_place = lax.cummax(changes * places, axis=segment_rows.ndim - 1)
    position = (places - first_place).astype(jnp.float32)
    exponent = jnp.arange(0, ROT, 2).astype(jnp.float32) / ROT
    frequency = 1.0 / jnp.power(10000.0, exponent)
    angles = position[..., None] * frequency
    angles = jnp.concatenate([angles, angles], axis=-1)
    return (jnp.cos(angles), jnp.sin(angles))


def rotate(heads_part, cos_table, sin_table):
    half_rot = ROT // 2
    turned = heads_part[..., :ROT]
    swapped = jnp.concatenate([-turned[..., half_rot:], turned[..., :half_rot]], axis=-1)
    turned = turned * cos_table[..., None, :] + swapped * sin_table[..., None, :]
    return jnp.concatenate([turned, heads_part[..., ROT:]], axis=-1)


def unrotate(grads_part, cos_table, sin_table):
    half_rot = ROT // 2
    turned = grads_part[..., :ROT]
    along_sin = turned * sin_table[..., None, :]
    back_turn = jnp.concatenate([along_sin[..., half_rot:], -along_sin[..., :half_rot]], axis=-1)
    turned = turned * cos_table[..., None, :] + back_turn
    return jnp.concatenate([turned, grads_part[..., ROT:]], axis=-1)


def build_mask(segment_row):
    places = jnp.arange(segment_row.shape[0], dtype=jnp.int32)
    return (segment_row[:, None] == segment_row[None, :]) & (places[None, :] <= places[:, None])


def attend_forward(scanned):
    queries, keys_rot, values, segment_row = scanned
    scores = jnp.einsum("qhd,khd->hqk", queries, keys_rot, preferred_element_type=jnp.float32) * (
        1.0 / math.sqrt(HEAD_DIM)
    )
    scores = jnp.where(build_mask(segment_row)[None], scores, NEGATIVE)
    row_top = jnp.max(scores, axis=-1, keepdims=True)
    exponent = jnp.exp(scores - row_top)
    row_total = jnp.sum(exponent, axis=-1, keepdims=True)
    attention = (exponent / row_total).astype(jnp.bfloat16)
    context = jnp.einsum("hqk,khd->qhd", attention, values, preferred_element_type=jnp.float32)
    return (context.astype(jnp.bfloat16), row_top + jnp.log(row_total))


def attend_backward(scanned):
    queries, keys_rot, values, segment_row, log_total, context_grad = scanned
    scale_factor = 1.0 / math.sqrt(HEAD_DIM)
    scores = (
        jnp.einsum("qhd,khd->hqk", queries, keys_rot, preferred_element_type=jnp.float32)
        * scale_factor
    )
    attention = jnp.where(build_mask(segment_row)[None], jnp.exp(scores - log_total), 0.0)
    value_grad = jnp.einsum(
        "hqk,qhd->khd",
        attention.astype(jnp.bfloat16),
        context_grad,
        preferred_element_type=jnp.float32,
    )
    attention_grad = jnp.einsum(
        "qhd,khd->hqk", context_grad, values, preferred_element_type=jnp.float32
    )
    row_centre = jnp.sum(attention * attention_grad, axis=-1, keepdims=True)
    score_grad = (attention * (attention_grad - row_centre)).astype(jnp.bfloat16)
    query_grad = (
        jnp.einsum("hqk,khd->qhd", score_grad, keys_rot, preferred_element_type=jnp.float32)
        * scale_factor
    )
    key_grad = (
        jnp.einsum("hqk,qhd->khd", score_grad, queries, preferred_element_type=jnp.float32)
        * scale_factor
    )
    return (query_grad, key_grad, value_grad)


def per_device(
    hidden_in,
    segments,
    ln1_gain,
    ln1_bias,
    ln2_gain,
    ln2_bias,
    w_qkv,
    b_qkv,
    w_dense,
    b_dense,
    w_up,
    b_up,
    w_down,
    b_down,
    cotangent,
):
    seq_count, shard_len, width = hidden_in.shape
    tok_rows = seq_count * shard_len
    inputs = hidden_in.reshape(tok_rows, width).astype(jnp.float32)
    upstream = cotangent.reshape(tok_rows, width)
    upstream_f32 = upstream.astype(jnp.float32)
    full_qkv, full_dense = (
        lax.all_gather(w_qkv, "fsdp", axis=0, tiled=True),
        lax.all_gather(w_dense, "fsdp", axis=0, tiled=True),
    )
    normed, scaled_attn, inverse_attn = norm_forward(inputs, ln1_gain, ln1_bias)
    normed = normed.astype(jnp.bfloat16)
    packed = (times_transposed(normed, full_qkv) + b_qkv).astype(jnp.bfloat16)
    packed = packed.reshape(seq_count, shard_len, HEADS, 3 * HEAD_DIM)
    by_head = lax.all_to_all(packed, "sp", split_axis=2, concat_axis=1, tiled=True)
    cos_table, sin_table = rotary_tables(segments)
    queries = rotate(by_head[..., :HEAD_DIM].astype(jnp.float32), cos_table, sin_table).astype(
        jnp.bfloat16
    )
    keys_rot = rotate(
        by_head[..., HEAD_DIM : 2 * HEAD_DIM].astype(jnp.float32), cos_table, sin_table
    ).astype(jnp.bfloat16)
    values = by_head[..., 2 * HEAD_DIM :]
    context, log_total = lax.map(attend_forward, (queries, keys_rot, values, segments))
    merged = lax.all_to_all(context, "sp", split_axis=1, concat_axis=2, tiled=True).reshape(
        tok_rows, width
    )
    attended = times_transposed(merged, full_dense) + b_dense
    normed_mlp, scaled_mlp, inverse_mlp = norm_forward(inputs, ln2_gain, ln2_bias)
    normed_mlp = normed_mlp.astype(jnp.bfloat16)
    full_up, full_down = (
        lax.all_gather(w_up, "fsdp", axis=0, tiled=True),
        lax.all_gather(w_down, "fsdp", axis=0, tiled=True),
    )
    hidden = times_transposed(normed_mlp, full_up) + b_up
    activated, slope = gelu_pair(hidden)
    activated = activated.astype(jnp.bfloat16)
    mlp_out = jnp.dot(activated, full_down, preferred_element_type=jnp.float32) + b_down
    hidden_grad = (times_transposed(upstream, full_down) * slope).astype(jnp.bfloat16)
    mlp_in_grad = jnp.dot(hidden_grad, full_up, preferred_element_type=jnp.float32)
    grad_cols = hidden_grad
    mlp_shard = lax.psum_scatter(
        jnp.concatenate(
            [contract_rows(grad_cols, normed_mlp), contract_rows(activated, upstream)], axis=1
        ),
        "fsdp",
        scatter_dimension=0,
        tiled=True,
    )
    up_grad = mlp_shard[:, :width]
    down_grad = mlp_shard[:, width:]
    bias_up = jnp.sum(hidden_grad.astype(jnp.float32), axis=0)
    output = (inputs + attended + mlp_out).astype(jnp.bfloat16).reshape(seq_count, shard_len, width)
    dense_in_grad = jnp.dot(upstream, full_dense, preferred_element_type=jnp.float32).astype(
        jnp.bfloat16
    )
    context_grad = lax.all_to_all(
        dense_in_grad.reshape(seq_count, shard_len, HEADS, HEAD_DIM),
        "sp",
        split_axis=2,
        concat_axis=1,
        tiled=True,
    )
    query_grad, key_grad, value_grad = lax.map(
        attend_backward, (queries, keys_rot, values, segments, log_total, context_grad)
    )
    packed_grad = jnp.concatenate(
        [
            unrotate(query_grad, cos_table, sin_table),
            unrotate(key_grad, cos_table, sin_table),
            value_grad,
        ],
        axis=-1,
    ).astype(jnp.bfloat16)
    packed_grad = lax.all_to_all(
        packed_grad, "sp", split_axis=1, concat_axis=2, tiled=True
    ).reshape(tok_rows, 3 * width)
    normed_grad = jnp.dot(packed_grad, full_qkv, preferred_element_type=jnp.float32)
    qkv_part = w_qkv.shape[0]
    dense_part = w_dense.shape[0]
    block_size = qkv_part + dense_part
    block_total = lax.axis_size("fsdp") * block_size // block_size
    grad_cols = packed_grad
    qkv_term = contract_rows(grad_cols, normed).reshape(block_total, qkv_part, width)
    dense_term = contract_rows(upstream, merged).reshape(block_total, dense_part, width)
    attn_shard = lax.psum_scatter(
        jnp.concatenate([qkv_term, dense_term], axis=1).reshape(
            lax.axis_size("fsdp") * block_size, width
        ),
        "fsdp",
        scatter_dimension=0,
        tiled=True,
    )
    qkv_local = attn_shard[:qkv_part]
    dense_local = attn_shard[qkv_part:]
    grad_qkv_w, grad_dense_w, grad_up_w, grad_down_w = lax.psum(
        (qkv_local, dense_local, up_grad, down_grad), "sp"
    )
    attn_input, gain_one, shift_one = norm_backward(
        normed_grad, scaled_attn, inverse_attn, ln1_gain
    )
    mlp_input, gain_two, shift_two = norm_backward(mlp_in_grad, scaled_mlp, inverse_mlp, ln2_gain)
    input_grad = (
        (upstream_f32 + attn_input + mlp_input)
        .astype(jnp.bfloat16)
        .reshape(seq_count, shard_len, width)
    )
    bias_out = jnp.sum(upstream_f32, axis=0)
    bias_qkv = jnp.sum(packed_grad.astype(jnp.float32), axis=0)
    summed = lax.psum(
        (gain_one, shift_one, gain_two, shift_two, bias_qkv, bias_out, bias_up), ("fsdp", "sp")
    )
    fsdp_index = lax.axis_index("fsdp")
    fsdp_count = lax.axis_size("fsdp")

    def own_part(vector):
        piece_len = vector.shape[0] // fsdp_count
        return lax.dynamic_slice_in_dim(vector, fsdp_index * piece_len, piece_len, 0)

    bias_out_part = own_part(summed[5])
    return (
        output,
        input_grad,
        own_part(summed[0]),
        own_part(summed[1]),
        own_part(summed[2]),
        own_part(summed[3]),
        grad_qkv_w,
        own_part(summed[4]),
        grad_dense_w,
        bias_out_part,
        grad_up_w,
        own_part(summed[6]),
        grad_down_w,
        bias_out_part,
    )


def solution(mesh):
    return jax.shard_map(
        per_device,
        mesh=mesh,
        in_specs=(
            P("fsdp", "sp", None),
            P("fsdp", None),
            P(),
            P(),
            P(),
            P(),
            P("fsdp", None),
            P(),
            P("fsdp", None),
            P(),
            P("fsdp", None),
            P(),
            P("fsdp", None),
            P(),
            P("fsdp", "sp", None),
        ),
        out_specs=(
            P("fsdp", "sp", None),
            P("fsdp", "sp", None),
            P("fsdp"),
            P("fsdp"),
            P("fsdp"),
            P("fsdp"),
            P("fsdp", None),
            P("fsdp"),
            P("fsdp", None),
            P("fsdp"),
            P("fsdp", None),
            P("fsdp"),
            P("fsdp", None),
            P("fsdp"),
        ),
        check_vma=False,
    )
```

profile of v0, /device:TPU:0, one launch (start us, length us, event | category | flops | bytes accessed | tf_op | source)
XLA Modules:
  0.0 2658.6 jit_solution(7697553967098281096)
XLA Ops:
  10.7 56.3 %all-gather.7.cloned.1.call-done = bf16[2048,2048]{1,0:T(8,128)(2,1)} async-done(((bf16[256,2048]{1,0:T(8,128)(2,1)}), bf16[2048,2048]{1,0:T(8,128)(2,1)}) %all-gather.7.cloned.1.call-update) | async-done | bytes 8388624 | tf_op jit(solution)/shard_map/all_gather | solution.py:162
  67.0 5.7 convolution_convert_fusion
  74.3 4.6 all-to-all-start.2
  78.9 115.4 %all-gather.5.cloned.1.call-done = bf16[6144,2048]{1,0:T(8,128)(2,1)} async-done(((bf16[768,2048]{1,0:T(8,128)(2,1)}), bf16[6144,2048]{1,0:T(8,128)(2,1)}) %all-gather.5.cloned.1.call-update) | async-done | bytes 25165840 | tf_op jit(solution)/shard_map/all_gather | solution.py:161
  194.3 12.9 fusion.5
  207.1 3.3 copy.178
  210.4 2.3 copy.141
  213.7 5.0 all-to-all-start
  219.9 2.9 fusion.90
  222.8 1.6 fusion.13
  224.4 2.3 copy.149
  226.6 63.2 %all-to-all-done = bf16[1,256,8,768]{3,1,0,2:T(8,128)(2,1)S(1)} async-done(((bf16[1,256,8,768]{3,1,0,2:T(8,128)(2,1)}), bf16[1,256,8,768]{3,1,0,2:T(8,128)(2,1)S(1)}, u32[]{:S(2)}, u32[]{:S(2)}) %all-to-all-start) | async-done | bytes 3145760 | tf_op jit(solution)/shard_map/all_to_all | solution.py:168
  289.8 1.7 copy-done.8
  291.5 2.1 copy.142
  297.8 2.5 select_reduce_fusion
  300.3 2.0 fusion.6
  302.3 1.4 copy-done
  303.7 4.0 fusion.60
  307.7 3.7 copy.145
  311.4 4.4 all-to-all-start.1
  315.9 5.8 multiply_reduce_fusion
  322.8 2.6 multiply_convert_fusion
  325.4 2.0 copy-done.6
  327.4 2.1 multiply_bitcast_fusion.1
  331.2 4.5 multiply_bitcast_fusion
  337.1 1.3 slice.176
  338.5 2.2 copy.161
  340.7 1.4 slice_multiply_fusion.2
  343.8 1.4 fusion.70
  345.2 1.4 copy.160
  347.4 1.8 constant_dynamic-update-slice_fusion.3
  351.8 7.4 fusion.57
  359.1 8.8 copy.162
  368.0 5.2 all-to-all-start.3
  373.2 1.6 copy.146
  375.5 8.1 fusion.73
  383.6 59.0 %all-to-all-done.3 = bf16[1,1024,2,768]{3,2,0,1:T(2,128)(2,1)} async-done(((bf16[1,1024,2,768]{3,2,0,1:T(2,128)(2,1)}), bf16[1,1024,2,768]{3,2,0,1:T(2,128)(2,1)}, u32[]{:S(2)}, u32[]{:S(2)}) %all-to-all-start.3) | async-done | bytes 3145760 | tf_op jit(solution)/shard_map/all_to_all | solution.py:228
  442.7 2.3 copy.163
  445.0 3.2 copy.164
  448.2 21.9 fusion.62
  470.1 45.9 %pad_maximum_fusion.1 = f32[8,1024,2048]{2,1,0:T(8,128)} fusion(f32[8,256,2048]{2,1,0:T(8,128)} %bitcast.181, f32[8,768,2048]{2,1,0:T(8,128)} %fusion.62), kind=kLoop, calls=%fused_computation.1 | loop fusion | flops 16777216 | bytes 134217728 | tf_op jit(solution)/shard_map/concatenate | solution.py:240
  517.4 20.7 convolution_add_fusion
  538.1 27.3 %convert_reduce_fusion = (f32[8192]{0:T(1024)}, bf16[256,8192]{1,0:T(8,128)(2,1)}) fusion(f32[256,8192]{1,0:T(8,128)} %convolution_add_fusion, bf16[8192,2048]{1,0:T(8,128)(2,1)} %all-gather.11.cloned.1.call-done, bf16[1,256,2048]{2,1,0:T(8,128)(2,1)S(1)} %copy-done.11), kind=kOutput, calls=%fused_computation.10 | convolution fusion | flops 8615092224 | bytes 47218688 | tf_op jit(solution)/shard_map/dot_general | solution.py:23
  565.4 40.8 %fusion.101 = f32[8192,2048]{0,1:T(8,128)} fusion(bf16[256,8192]{1,0:T(8,128)(2,1)} %get-tuple-element.202, bf16[1,256,2048]{2,1,0:T(8,128)(2,1)S(1)} %copy-done.4, f32[2048]{0:T(1024)S(1)} %copy-done.45, f32[2048]{0:T(1024)S(1)} %copy-done.38, f32[256]{0:T(256)S(1)} %add_rsqrt_fusion, f32[256]{0:T(256)S(1)} %broadcast_multiply_fusion.5), kind=kOutput, calls=%fused_computation.162 | convolution fusion | flops 8593080320 | bytes 72370176 | tf_op jit(solution)/shard_map/dot_general | solution.py:17
  606.2 29.2 %fusion.71 = f32[8192,2048]{0,1:T(8,128)} fusion(bf16[1,256,2048]{2,1,0:T(8,128)(2,1)S(1)} %copy-done.11, f32[256,8192]{1,0:T(8,128)} %convolution_add_fusion), kind=kOutput, calls=%fused_computation.110 | convolution fusion | flops 8600420352 | bytes 76546048 | tf_op jit(solution)/shard_map/dot_general | solution.py:17
  635.5 90.6 %pad_maximum_fusion = f32[8192,4096]{0,1:T(8,128)} fusion(f32[8192,2048]{0,1:T(8,128)} %fusion.71, f32[8192,2048]{0,1:T(8,128)} %fusion.101), kind=kLoop, calls=%fused_computation | loop fusion | flops 33554432 | bytes 268435456 | tf_op jit(solution)/shard_map/concatenate | solution.py:196
  726.2 2.0 copy-done.2
  729.3 17.5 fusion.107
  746.9 13.7 fusion.43
  760.7 3.1 convert_reduce_fusion.3
  763.9 142.9 %reduce-scatter.3.cloned.1.call-done = f32[1024,2048]{1,0:T(8,128)} async-done(((f32[8192,2048]{1,0:T(8,128)}), f32[1024,2048]{1,0:T(8,128)}) %reduce-scatter.3.cloned.1.call-update) | async-done | bytes 8388624 | tf_op jit(solution)/shard_map/reduce_scatter | solution.py:239
  906.8 3.1 slice.138
  909.9 6.3 slice.137
  916.2 735.3 %reduce-scatter.5.cloned.1.call-done = f32[1024,4096]{0,1:T(8,128)} async-done(((f32[8192,4096]{0,1:T(8,128)}), f32[1024,4096]{0,1:T(8,128)}) %reduce-scatter.5.cloned.1.call-update) | async-done | bytes 16777232 | tf_op jit(solution)/shard_map/reduce_scatter | solution.py:195
  1651.5 11.3 fusion.104
  1664.0 7.1 fusion.16
  1671.2 23.5 fusion.30
  1694.7 88.5 %all-reduce.5.cloned.1.call-done = (f32[2048]{0:T(1024)}, f32[2048]{0:T(1024)}, f32[2048]{0:T(1024)}, f32[2048]{0:T(1024)}, f32[6144]{0:T(1024)}, /*index=5*/f32[2048]{0:T(1024)}, f32[8192]{0:T(1024)}) async-done(((f32[2048]{0:T(1024)}, f32[2048]{0:T(1024)}, f32[2048]{0:T(1024)}, f32[2048]{0:T(1024)}, f32[6144]{0:T(1024)}, /*index=5*/f32[2048]{0:T(1024)}, f32[8192]{0:T(1024)}), (f32[2048]{0:T(1024)}, ...) | async-done | bytes 98320 | tf_op jit(solution)/shard_map/psum | solution.py:263
  1789.1 1.4 dynamic_slice.48
  1791.8 833.2 %all-reduce.7.cloned.1.call-done = (f32[768,2048]{1,0:T(8,128)}, f32[256,2048]{1,0:T(8,128)}, f32[1024,2048]{0,1:T(8,128)}, f32[1024,2048]{0,1:T(8,128)}) async-done(((f32[768,2048]{1,0:T(8,128)}, f32[256,2048]{1,0:T(8,128)}, f32[1024,2048]{0,1:T(8,128)}, f32[1024,2048]{0,1:T(8,128)}), (f32[768,2048]{1,0:T(8,128)}, f32[256,2048]{1,0:T(8,128)}, f32[1024,2048]{0,1:T(8,128)}, ...) | async-done | bytes 25165840 | tf_op jit(solution)/shard_map/psum | solution.py:249
  2625.0 9.1 copy.166
  2634.1 9.1 copy.167
  2643.8 6.4 copy.197
  2650.2 1.3 copy.198
  (168 shorter events, 32.8 us)
Async XLA Ops:
  7.2 59.8 %all-gather.7.cloned.1.call-start = ((), (), s32[]{:S(2)}) async-start(), calls=%async_computation.7 | async-start | bytes 9437184 | tf_op jit(solution)/shard_map/all_gather | solution.py:162
  7.9 186.4 %all-gather.5.cloned.1.call-start = ((), (), s32[]{:S(2)}) async-start(), calls=%async_computation.6 | async-start | bytes 28311552 | tf_op jit(solution)/shard_map/all_gather | solution.py:161
  8.7 1.3 copy-start.3
  8.7 507.5 %all-gather.9.cloned.1.call-start = ((), (), s32[]{:S(2)}) async-start(), calls=%async_computation.8 | async-start | bytes 37748736 | tf_op jit(solution)/shard_map/all_gather | solution.py:185
  9.4 57.6 %copy-start.9 = (bf16[1,256,2048]{2,1,0:T(8,128)(2,1)S(1)}, bf16[1,256,2048]{2,1,0:T(8,128)(2,1)}, u32[]{:S(2)}) copy-start(bf16[1,256,2048]{2,1,0:T(8,128)(2,1)} %param.29) | copy-start | bytes 3145732
  9.4 528.6 %all-gather.11.cloned.1.call-start = ((), (), s32[]{:S(2)}) async-start(), calls=%async_computation.9 | async-start | bytes 37748736 | tf_op jit(solution)/shard_map/all_gather | solution.py:186
  10.2 555.2 %copy-start.40 = (f32[256]{0:T(256)}, f32[256]{0:T(256)S(1)}, u32[]{:S(2)}) copy-start(f32[256]{0:T(256)S(1)} %broadcast_multiply_fusion.5) | copy-start | bytes 3076
  10.7 554.7 %copy-start.42 = (f32[256]{0:T(256)}, f32[256]{0:T(256)S(1)}, u32[]{:S(2)}) copy-start(f32[256]{0:T(256)S(1)} %add_rsqrt_fusion) | copy-start | bytes 3076
  72.7 121.5 %copy-start.36 = (f32[2048]{0:T(1024)S(1)}, f32[2048]{0:T(1024)}, u32[]{:S(2)}) copy-start(f32[2048]{0:T(1024)} %param.17) | copy-start | bytes 24580
  72.8 121.5 %copy-start.44 = (f32[2048]{0:T(1024)S(1)}, f32[2048]{0:T(1024)}, u32[]{:S(2)}) copy-start(f32[2048]{0:T(1024)} %param.18) | copy-start | bytes 24580
  72.8 121.5 %copy-start.48 = (f32[6144]{0:T(1024)S(1)}, f32[6144]{0:T(1024)}, u32[]{:S(2)}) copy-start(f32[6144]{0:T(1024)} %param.22) | copy-start | bytes 73732
  74.3 138.4 %all-to-all-start.2 = ((bf16[1,256,8,256]{3,1,0,2:T(8,128)(2,1)}), bf16[1,256,8,256]{3,1,0,2:T(8,128)(2,1)S(1)}, u32[]{:S(2)}, u32[]{:S(2)}) async-start(bf16[1,256,8,256]{3,1,0,2:T(8,128)(2,1)} %copy.148), calls=%async_computation.2 | async-start | bytes 2097152 | tf_op jit(solution)/shard_map/all_to_all | solution.py:210
  212.7 6.0 copy-start.35
  213.7 76.1 %all-to-all-start = ((bf16[1,256,8,768]{3,1,0,2:T(8,128)(2,1)}), bf16[1,256,8,768]{3,1,0,2:T(8,128)(2,1)S(1)}, u32[]{:S(2)}, u32[]{:S(2)}) async-start(bf16[1,256,8,768]{3,1,0,2:T(8,128)(2,1)} %copy.141), calls=%async_computation | async-start | bytes 6291456 | tf_op jit(solution)/shard_map/all_to_all | solution.py:168
  289.8 1.7 copy-start.8
  294.6 2.6 copy-start.25
  294.6 2.6 copy-start.33
  295.0 1.4 copy-start.16
  295.0 1.6 copy-start.20
  296.6 1.2 copy-start.13
  297.2 3.0 copy-start.30
  297.2 3.0 copy-start.34
  300.3 3.4 copy-start
  311.4 56.5 %all-to-all-start.1 = ((bf16[1,1024,2,256]{3,2,0,1:T(2,128)(2,1)}), bf16[1,1024,2,256]{3,2,0,1:T(2,128)(2,1)}, u32[]{:S(2)}, u32[]{:S(2)}) async-start(bf16[1,1024,2,256]{3,2,0,1:T(2,128)(2,1)} %copy.145), calls=%async_computation.1 | async-start | bytes 2097152 | tf_op jit(solution)/shard_map/all_to_all | solution.py:178
  315.9 5.8 slice-start
  315.9 6.7 slice-start.1
  315.9 6.9 copy-start.14
  322.8 4.6 copy-start.26
  322.8 4.6 copy-start.31
  325.4 2.0 copy-start.6
  331.2 9.4 copy-start.17
  335.8 1.3 copy-start.18
  342.0 1.6 copy-start.19
  342.1 1.7 copy-start.21
  343.8 5.4 copy-start.27
  345.1 5.7 copy-start.28
  345.1 6.6 copy-start.15
  347.4 4.4 copy-start.32
  368.0 7.5 copy-start.10
  368.0 74.7 %all-to-all-start.3 = ((bf16[1,1024,2,768]{3,2,0,1:T(2,128)(2,1)}), bf16[1,1024,2,768]{3,2,0,1:T(2,128)(2,1)}, u32[]{:S(2)}, u32[]{:S(2)}) async-start(bf16[1,1024,2,768]{3,2,0,1:T(2,128)(2,1)} %copy.162), calls=%async_computation.3 | async-start | bytes 6291456 | tf_op jit(solution)/shard_map/all_to_all | solution.py:228
  373.2 533.6 %reduce-scatter.3.cloned.1.call-start = ((), (), s32[]{:S(2)}) async-start(), calls=%async_computation.10 | async-start | bytes 75497472 | tf_op jit(solution)/shard_map/reduce_scatter | solution.py:239
  375.5 8.1 copy-start.22
  445.0 25.2 copy-start.1
  516.1 1.3 copy-start.4
  516.1 1.3 copy-start.38
  516.1 1.3 copy-start.45
  516.1 1.3 copy-start.47
  516.1 21.9 copy-start.11
  516.1 1135.4 %reduce-scatter.5.cloned.1.call-start = ((), (), s32[]{:S(2)}) async-start(), calls=%async_computation.11 | async-start | bytes 150994944 | tf_op jit(solution)/shard_map/reduce_scatter | solution.py:195
  726.1 2.1 copy-start.2
  726.1 1057.0 %all-reduce.5.cloned.1.call-start = ((), (), s32[]{:S(2)}) async-start(), calls=%async_computation.12 | async-start | bytes 196608 | tf_op jit(solution)/shard_map/psum | solution.py:263
  729.3 17.5 copy-start.5
  729.3 17.6 copy-start.7
  729.3 17.6 copy-start.37
  729.3 17.6 copy-start.39
  729.3 17.6 copy-start.41
  729.3 17.6 copy-start.43
  746.9 13.8 copy-start.12
  763.8 1861.1 %all-reduce.7.cloned.1.call-start = ((), (), s32[]{:S(2)}) async-start(), calls=%async_computation.13 | async-start | bytes 50331648 | tf_op jit(solution)/shard_map/psum | solution.py:249
  1662.8 1.2 copy-start.23
  1662.8 1.2 copy-start.49
  1664.0 7.1 copy-start.50
  1785.2 858.0 %copy-start.46 = (f32[256]{0:T(256)}, f32[256]{0:T(256)S(1)}, u32[]{:S(2)}) copy-start(f32[256]{0:T(256)S(1)} %dynamic_slice.49) | copy-start | bytes 3076
  2643.8 6.4 copy-start.29
  (1 other events, 1.0 us)
Sparse Core Ops, SparseCore 0:
  9.9 57.0 all-gather.6
  68.9 125.3 all-gather.4
  196.2 160.7 all-gather.8
  358.7 160.8 all-gather.10
  523.0 383.7 reduce-scatter.2
  910.6 740.8 reduce-scatter.4
  1659.1 124.0 all-reduce.4
  1787.2 837.7 all-reduce.6
where the time goes:
time: 2670 us; the launch traced here: 2660 us
  waiting for transfers between devices  2100 us (79%)
  matrix products  255 us (10%)
  other arithmetic  156 us (6%)
  local copies, waits for them, and re-layouts  117 us (4%)
    psum x1, waiting for transfers between devices, per_device(): lax.psum((qkv_local, dense_local, up_grad, down_grad), 'sp')  833 us
    reduce_scatter x1, waiting for transfers between devices, per_device(): lax.psum_scatter(jnp.concatenate([contract_rows(grad_cols, normed_mlp), c...  735 us
    reduce_scatter x1, waiting for transfers between devices, per_device(): lax.psum_scatter(jnp.concatenate([qkv_term, dense_term], axis=1).reshape(...  143 us
    all_gather x1, waiting for transfers between devices, per_device(): lax.all_gather(w_qkv, 'fsdp', axis=0, tiled=True)  115 us
    dot_general x4, matrix products, contract_rows(): lax.dot_general(former, latter, (((0,), (0,)), ((), ())), preferred_eleme...  100 us
    concatenate x1, other arithmetic, per_device(): jnp.concatenate([contract_rows(grad_cols, normed_mlp), contract_rows(acti...  90.6 us
    psum x1, waiting for transfers between devices, per_device(): lax.psum((gain_one, shift_one, gain_two, shift_two, bias_qkv, bias_out, b...  88.5 us
    dot_general x4, matrix products, times_transposed(): lax.dot_general(former, latter, (((1,), (1,)), ((), ())), preferred_eleme...  68 us
  transfers between devices with their start and end apart: 12, of which 8 were waited for; matrix products, arithmetic and copies ran while one was open for 18% of the time, Pallas kernels for 0%

commit v1 on v0

--- a/solution.py
+++ b/solution.py
@@ -11,6 +11,18 @@
 NEGATIVE = -1e30
 ROOT_HALF = 0.7071067811865476
 ROOT_TWO_PI = 2.5066282746310002
+
+
+def doubled_up(x, axis, dim):
+    ways, here, step = (lax.axis_size(axis), lax.axis_index(axis), x.shape[dim])
+    line, have = (x, 1)
+    while have < ways:
+        line = jnp.concatenate(
+            [line, lax.ppermute(line, axis, [(d, (d - have) % ways) for d in range(ways)])],
+            axis=dim,
+        )
+        have = 2 * have
+    return jnp.roll(line, here * step, axis=dim)
 
 
 def contract_rows(former, latter):
@@ -159,7 +171,7 @@
     upstream_f32 = upstream.astype(jnp.float32)
     full_qkv, full_dense = (
         lax.all_gather(w_qkv, "fsdp", axis=0, tiled=True),
-        lax.all_gather(w_dense, "fsdp", axis=0, tiled=True),
+        doubled_up(w_dense, "fsdp", 0),
     )
     normed, scaled_attn, inverse_attn = norm_forward(inputs, ln1_gain, ln1_bias)
     normed = normed.astype(jnp.bfloat16)

time: 2670 us -> 2760 us (1.034)
  waiting for transfers between devices: 2100 us -> 2170 us
    ppermute x0 -> x3, waiting for transfers between devices: none -> 248 us  [doubled_up(): lax.ppermute(line, axis, [(d, (d - have) % ways) for d in range(ways)])]
    all_gather x1, waiting for transfers between devices: 115 us -> 0.01 us  [per_device(): lax.all_gather(w_qkv, 'fsdp', axis=0, tiled=True)]
    all_gather x1 -> x0, waiting for transfers between devices: 56.3 us -> none  [per_device(): lax.all_gather(w_dense, 'fsdp', axis=0, tiled=True)]
    unnamed x117 -> x133, local copies, waits for them, and re-layouts: 49.9 us -> 55.5 us
  transfers between devices with their start and end apart: 12 -> 14, of which waited for: 8 -> 10; matrix products, arithmetic and copies ran while one was open for 18% -> 18% of each run, Pallas kernels for 0% -> 0%
where the time goes in v1:
time: 2760 us; the launch traced here: 2750 us
  waiting for transfers between devices  2170 us (79%)
  matrix products  257 us (9%)
  other arithmetic  158 us (6%)
  local copies, waits for them, and re-layouts  124 us (4%)
    psum x1, waiting for transfers between devices, per_device(): lax.psum((qkv_local, dense_local, up_grad, down_grad), 'sp')  833 us
    reduce_scatter x1, waiting for transfers between devices, per_device(): lax.psum_scatter(jnp.concatenate([contract_rows(grad_cols, normed_mlp), c...  735 us
    ppermute x3, waiting for transfers between devices, doubled_up(): lax.ppermute(line, axis, [(d, (d - have) % ways) for d in range(ways)])  248 us
    reduce_scatter x1, waiting for transfers between devices, per_device(): lax.psum_scatter(jnp.concatenate([qkv_term, dense_term], axis=1).reshape(...  134 us
    dot_general x4, matrix products, contract_rows(): lax.dot_general(former, latter, (((0,), (0,)), ((), ())), preferred_eleme...  100 us
    concatenate x1, other arithmetic, per_device(): jnp.concatenate([contract_rows(grad_cols, normed_mlp), contract_rows(acti...  91.1 us
    psum x1, waiting for transfers between devices, per_device(): lax.psum((gain_one, shift_one, gain_two, shift_two, bias_qkv, bias_out, b...  88.6 us
    dot_general x4, matrix products, times_transposed(): lax.dot_general(former, latter, (((1,), (1,)), ((), ())), preferred_eleme...  70.7 us
  transfers between devices with their start and end apart: 14, of which 10 were waited for; matrix products, arithmetic and copies ran while one was open for 18% of the time, Pallas kernels for 0%

profile of v1, /device:TPU:0, one launch (start us, length us, event | category | flops | bytes accessed | tf_op | source)
XLA Modules:
  0.0 2746.5 jit_solution(5606445623455034644)
XLA Ops:
  9.4 3.4 collective-permute-start
  12.8 15.6 collective-permute-done
  28.7 75.6 %collective-permute-done.1 = bf16[512,2048]{1,0:T(8,128)(2,1)S(1)} collective-permute-done((bf16[512,2048]{1,0:T(8,128)(2,1)S(1)}, bf16[512,2048]{1,0:T(8,128)(2,1)S(1)}, u32[]{:S(2)}, u32[]{:S(2)}) %collective-permute-start.1) | collective-permute-done | bytes 2097184 | tf_op jit(solution)/shard_map/ppermute | solution.py:21
  104.2 3.3 pad_maximum_fusion.2
  110.3 157.1 %collective-permute-done.2 = bf16[1024,2048]{1,0:T(8,128)(2,1)} collective-permute-done((bf16[1024,2048]{1,0:T(8,128)(2,1)}, bf16[1024,2048]{1,0:T(8,128)(2,1)}, u32[]{:S(2)}, u32[]{:S(2)}) %collective-permute-start.2) | collective-permute-done | bytes 4194336 | tf_op jit(solution)/shard_map/ppermute | solution.py:21
  267.4 3.5 constant_dynamic-update-slice_fusion.4
  271.2 2.6 constant_dynamic-update-slice_fusion
  273.9 4.3 fusion.30
  278.2 1.7 copy-done.40
  279.9 4.9 all-to-all-start.2
  284.8 12.9 fusion.5
  297.7 2.8 copy.178
  300.5 2.3 copy.141
  302.8 6.8 all-to-all-done.2
  310.5 4.2 all-to-all-start
  315.8 2.9 fusion.108
  318.8 1.6 fusion.17
  320.3 2.5 copy.149
  322.9 61.9 %all-to-all-done = bf16[1,256,8,768]{3,1,0,2:T(8,128)(2,1)S(1)} async-done(((bf16[1,256,8,768]{3,1,0,2:T(8,128)(2,1)}), bf16[1,256,8,768]{3,1,0,2:T(8,128)(2,1)S(1)}, u32[]{:S(2)}, u32[]{:S(2)}) %all-to-all-start) | async-done | bytes 3145760 | tf_op jit(solution)/shard_map/all_to_all | solution.py:180
  384.8 1.7 copy-done.12
  386.5 2.1 copy.142
  393.0 2.5 select_reduce_fusion
  395.5 2.0 fusion.10
  397.5 1.4 copy-done
  398.9 4.0 fusion.78
  402.9 3.7 copy.145
  406.6 4.4 all-to-all-start.1
  411.1 6.3 multiply_reduce_fusion
  418.3 2.6 multiply_convert_fusion
  420.9 2.0 copy-done.6
  422.9 2.1 multiply_bitcast_fusion.1
  426.7 5.0 multiply_bitcast_fusion
  434.4 2.2 copy.161
  443.3 1.8 constant_dynamic-update-slice_fusion.11
  447.6 6.9 fusion.75
  454.5 8.7 copy.162
  463.2 5.2 all-to-all-start.3
  470.5 8.1 fusion.91
  478.7 59.7 %all-to-all-done.3 = bf16[1,1024,2,768]{3,2,0,1:T(2,128)(2,1)} async-done(((bf16[1,1024,2,768]{3,2,0,1:T(2,128)(2,1)}), bf16[1,1024,2,768]{3,2,0,1:T(2,128)(2,1)}, u32[]{:S(2)}, u32[]{:S(2)}) %all-to-all-start.3) | async-done | bytes 3145760 | tf_op jit(solution)/shard_map/all_to_all | solution.py:240
  538.4 2.3 copy.163
  540.7 3.2 copy.164
  543.9 22.2 fusion.80
  566.2 44.0 %pad_maximum_fusion.1 = f32[8,1024,2048]{2,1,0:T(8,128)} fusion(f32[8,256,2048]{2,1,0:T(8,128)} %bitcast.187, f32[8,768,2048]{2,1,0:T(8,128)} %fusion.80), kind=kLoop, calls=%fused_computation.1 | loop fusion | flops 16777216 | bytes 134217728 | tf_op jit(solution)/shard_map/concatenate | solution.py:252
  611.3 23.0 convolution_add_fusion
  634.3 27.3 convert_reduce_fusion
  661.6 40.8 %fusion.121 = f32[8192,2048]{0,1:T(8,128)} fusion(bf16[256,8192]{1,0:T(8,128)(2,1)} %get-tuple-element.202, bf16[1,256,2048]{2,1,0:T(8,128)(2,1)S(1)} %copy-done.4, f32[2048]{0:T(1024)S(1)} %copy-done.50, f32[2048]{0:T(1024)S(1)} %copy-done.41, f32[256]{0:T(256)S(1)} %add_rsqrt_fusion, f32[256]{0:T(256)S(1)} %broadcast_multiply_fusion.5), kind=kOutput, calls=%fused_computation.178 | convolution fusion | flops 8593080320 | bytes 72370176 | tf_op jit(solution)/shard_map/dot_general | solution.py:29
  702.5 29.1 %fusion.89 = f32[8192,2048]{0,1:T(8,128)} fusion(bf16[1,256,2048]{2,1,0:T(8,128)(2,1)S(1)} %copy-done.15, f32[256,8192]{1,0:T(8,128)} %convolution_add_fusion), kind=kOutput, calls=%fused_computation.116 | convolution fusion | flops 8600420352 | bytes 76546048 | tf_op jit(solution)/shard_map/dot_general | solution.py:29
  731.5 91.1 %pad_maximum_fusion = f32[8192,4096]{0,1:T(8,128)} fusion(f32[8192,2048]{0,1:T(8,128)} %fusion.89, f32[8192,2048]{0,1:T(8,128)} %fusion.121), kind=kLoop, calls=%fused_computation | loop fusion | flops 33554432 | bytes 268435456 | tf_op jit(solution)/shard_map/concatenate | solution.py:208
  822.7 2.0 copy-done.2
  825.9 17.5 fusion.127
  843.4 13.8 fusion.61
  857.2 3.1 convert_reduce_fusion.3
  860.4 134.5 %reduce-scatter.3.cloned.1.call-done = f32[1024,2048]{1,0:T(8,128)} async-done(((f32[8192,2048]{1,0:T(8,128)}), f32[1024,2048]{1,0:T(8,128)}) %reduce-scatter.3.cloned.1.call-update) | async-done | bytes 8388624 | tf_op jit(solution)/shard_map/reduce_scatter | solution.py:251
  994.9 3.1 slice.138
  998.0 6.3 slice.137
  1004.3 735.3 %reduce-scatter.5.cloned.1.call-done = f32[1024,4096]{0,1:T(8,128)} async-done(((f32[8192,4096]{0,1:T(8,128)}), f32[1024,4096]{0,1:T(8,128)}) %reduce-scatter.5.cloned.1.call-update) | async-done | bytes 16777232 | tf_op jit(solution)/shard_map/reduce_scatter | solution.py:207
  1739.6 11.3 fusion.124
  1751.6 23.3 convolution_add_fusion.2
  1774.9 7.5 fusion.46
  1782.4 88.6 %all-reduce.5.cloned.1.call-done = (f32[2048]{0:T(1024)}, f32[2048]{0:T(1024)}, f32[2048]{0:T(1024)}, f32[2048]{0:T(1024)}, f32[6144]{0:T(1024)}, /*index=5*/f32[2048]{0:T(1024)}, f32[8192]{0:T(1024)}) async-done(((f32[2048]{0:T(1024)}, f32[2048]{0:T(1024)}, f32[2048]{0:T(1024)}, f32[2048]{0:T(1024)}, f32[6144]{0:T(1024)}, /*index=5*/f32[2048]{0:T(1024)}, f32[8192]{0:T(1024)}), (f32[2048]{0:T(1024)}, ...) | async-done | bytes 98320 | tf_op jit(solution)/shard_map/psum | solution.py:275
  1879.7 833.2 %all-reduce.7.cloned.1.call-done = (f32[768,2048]{1,0:T(8,128)}, f32[256,2048]{1,0:T(8,128)}, f32[1024,2048]{0,1:T(8,128)}, f32[1024,2048]{0,1:T(8,128)}) async-done(((f32[768,2048]{1,0:T(8,128)}, f32[256,2048]{1,0:T(8,128)}, f32[1024,2048]{0,1:T(8,128)}, f32[1024,2048]{0,1:T(8,128)}), (f32[768,2048]{1,0:T(8,128)}, f32[256,2048]{1,0:T(8,128)}, f32[1024,2048]{0,1:T(8,128)}, ...) | async-done | bytes 25165840 | tf_op jit(solution)/shard_map/psum | solution.py:261
  2712.9 9.1 copy.166
  2722.0 9.1 copy.167
  2731.7 6.4 copy.203
  (189 shorter events, 42.2 us)
Async XLA Ops:
  7.2 277.6 %all-gather.4.cloned.1.call-start = ((), (), s32[]{:S(2)}) async-start(), calls=%async_computation.6 | async-start | bytes 28311552 | tf_op jit(solution)/shard_map/all_gather | solution.py:173
  7.9 1.5 copy-start.7
  7.9 602.3 %all-gather.6.cloned.1.call-start = ((), (), s32[]{:S(2)}) async-start(), calls=%async_computation.7 | async-start | bytes 37748736 | tf_op jit(solution)/shard_map/all_gather | solution.py:197
  8.7 625.7 %all-gather.8.cloned.1.call-start = ((), (), s32[]{:S(2)}) async-start(), calls=%async_computation.8 | async-start | bytes 37748736 | tf_op jit(solution)/shard_map/all_gather | solution.py:198
  9.4 19.0 collective-permute-start
  28.4 79.1 %copy-start.9 = (bf16[256,2048]{1,0:T(8,128)(2,1)}, bf16[256,2048]{1,0:T(8,128)(2,1)S(1)}, u32[]{:S(2)}) copy-start(bf16[256,2048]{1,0:T(8,128)(2,1)S(1)} %collective-permute-done) | copy-start | bytes 3145732
  28.6 79.4 %copy-start.3 = (bf16[1,256,2048]{2,1,0:T(8,128)(2,1)S(1)}, bf16[1,256,2048]{2,1,0:T(8,128)(2,1)}, u32[]{:S(2)}) copy-start(bf16[1,256,2048]{2,1,0:T(8,128)(2,1)} %param.15) | copy-start | bytes 3145732
  28.6 75.6 %collective-permute-start.1 = (bf16[512,2048]{1,0:T(8,128)(2,1)S(1)}, bf16[512,2048]{1,0:T(8,128)(2,1)S(1)}, u32[]{:S(2)}, u32[]{:S(2)}) collective-permute-start(bf16[512,2048]{1,0:T(8,128)(2,1)S(1)} %pad_maximum_fusion.3), channel_id=1, source_target_pairs={{0,24},{4,28},{8,0},{12,4},{16,8},{20,12},{24,16},{28,20},{1,25},{... | collective-permute-start | bytes 6291464 | tf_op jit(solution)/shard_map/ppermute | solution.py:21
  107.5 159.9 %collective-permute-start.2 = (bf16[1024,2048]{1,0:T(8,128)(2,1)}, bf16[1024,2048]{1,0:T(8,128)(2,1)}, u32[]{:S(2)}, u32[]{:S(2)}) collective-permute-start(bf16[1024,2048]{1,0:T(8,128)(2,1)} %pad_maximum_fusion.2), channel_id=1, source_target_pairs={{0,16},{4,20},{8,24},{12,28},{16,0},{20,4},{24,8},{28,12},{1,17},{... | collective-permute-start | bytes 12582920 | tf_op jit(solution)/shard_map/ppermute | solution.py:21
  108.0 2.0 copy-start.10
  108.2 553.4 %copy-start.45 = (f32[256]{0:T(256)}, f32[256]{0:T(256)S(1)}, u32[]{:S(2)}) copy-start(f32[256]{0:T(256)S(1)} %broadcast_multiply_fusion.5) | copy-start | bytes 3076
  108.7 553.0 %copy-start.47 = (f32[256]{0:T(256)}, f32[256]{0:T(256)S(1)}, u32[]{:S(2)}) copy-start(f32[256]{0:T(256)S(1)} %add_rsqrt_fusion) | copy-start | bytes 3076
  110.2 160.6 %copy-start.8 = (bf16[256,2048]{1,0:T(8,128)(2,1)S(1)}, bf16[256,2048]{1,0:T(8,128)(2,1)}, u32[]{:S(2)}) copy-start(bf16[256,2048]{1,0:T(8,128)(2,1)} %param.23) | copy-start | bytes 3145732
  271.2 2.6 copy-start.13
  273.8 6.1 copy-start.40
  273.9 11.0 copy-start.43
  273.9 10.9 copy-start.49
  273.9 10.9 copy-start.53
  279.9 29.6 %all-to-all-start.2 = ((bf16[1,256,8,256]{1,3,0,2:T(8,128)(2,1)}), bf16[1,256,8,256]{1,3,0,2:T(8,128)(2,1)S(1)}, u32[]{:S(2)}, u32[]{:S(2)}) async-start(bf16[1,256,8,256]{1,3,0,2:T(8,128)(2,1)} %bitcast.23), calls=%async_computation.2 | async-start | bytes 2097152 | tf_op jit(solution)/shard_map/all_to_all | solution.py:222
  302.8 11.9 copy-start.39
  310.5 74.3 %all-to-all-start = ((bf16[1,256,8,768]{3,1,0,2:T(8,128)(2,1)}), bf16[1,256,8,768]{3,1,0,2:T(8,128)(2,1)S(1)}, u32[]{:S(2)}, u32[]{:S(2)}) async-start(bf16[1,256,8,768]{3,1,0,2:T(8,128)(2,1)} %copy.141), calls=%async_computation | async-start | bytes 6291456 | tf_op jit(solution)/shard_map/all_to_all | solution.py:180
  384.8 1.7 copy-start.12
  389.6 2.9 copy-start.29
  389.6 2.9 copy-start.37
  390.0 1.5 copy-start.20
  390.0 1.8 copy-start.24
  392.5 3.0 copy-start.34
  392.5 3.0 copy-start.38
  395.5 3.4 copy-start
  406.6 56.6 %all-to-all-start.1 = ((bf16[1,1024,2,256]{3,2,0,1:T(2,128)(2,1)}), bf16[1,1024,2,256]{3,2,0,1:T(2,128)(2,1)}, u32[]{:S(2)}, u32[]{:S(2)}) async-start(bf16[1,1024,2,256]{3,2,0,1:T(2,128)(2,1)} %copy.145), calls=%async_computation.1 | async-start | bytes 2097152 | tf_op jit(solution)/shard_map/all_to_all | solution.py:190
  411.0 6.3 slice-start
  411.0 7.0 slice-start.1
  411.1 7.2 copy-start.18
  418.3 4.6 copy-start.30
  418.3 4.6 copy-start.35
  420.9 2.0 copy-start.6
  426.7 9.9 copy-start.21
  437.9 1.6 copy-start.23
  437.9 1.7 copy-start.25
  439.6 5.4 copy-start.31
  441.0 5.7 copy-start.32
  441.0 6.6 copy-start.19
  443.3 4.4 copy-start.36
  463.2 7.3 copy-start.14
  463.2 75.2 %all-to-all-start.3 = ((bf16[1,1024,2,768]{3,2,0,1:T(2,128)(2,1)}), bf16[1,1024,2,768]{3,2,0,1:T(2,128)(2,1)}, u32[]{:S(2)}, u32[]{:S(2)}) async-start(bf16[1,1024,2,768]{3,2,0,1:T(2,128)(2,1)} %copy.162), calls=%async_computation.3 | async-start | bytes 6291456 | tf_op jit(solution)/shard_map/all_to_all | solution.py:240
  468.4 526.5 %reduce-scatter.3.cloned.1.call-start = ((), (), s32[]{:S(2)}) async-start(), calls=%async_computation.9 | async-start | bytes 75497472 | tf_op jit(solution)/shard_map/reduce_scatter | solution.py:251
  470.5 8.2 copy-start.26
  540.7 25.4 copy-start.1
  610.2 24.2 copy-start.15
  610.2 1129.4 %reduce-scatter.5.cloned.1.call-start = ((), (), s32[]{:S(2)}) async-start(), calls=%async_computation.10 | async-start | bytes 150994944 | tf_op jit(solution)/shard_map/reduce_scatter | solution.py:207
  822.6 2.1 copy-start.2
  822.7 1048.4 %all-reduce.5.cloned.1.call-start = ((), (), s32[]{:S(2)}) async-start(), calls=%async_computation.11 | async-start | bytes 196608 | tf_op jit(solution)/shard_map/psum | solution.py:275
  825.8 17.5 copy-start.5
  825.8 17.6 copy-start.11
  825.8 17.6 copy-start.42
  825.8 17.6 copy-start.44
  825.8 17.6 copy-start.46
  825.8 17.6 copy-start.48
  843.4 13.8 copy-start.16
  860.3 1852.5 %all-reduce.7.cloned.1.call-start = ((), (), s32[]{:S(2)}) async-start(), calls=%async_computation.12 | async-start | bytes 50331648 | tf_op jit(solution)/shard_map/psum | solution.py:261
  1751.6 23.3 copy-start.27
  1751.6 23.3 copy-start.55
  1873.1 858.0 %copy-start.51 = (f32[256]{0:T(256)}, f32[256]{0:T(256)S(1)}, u32[]{:S(2)}) copy-start(f32[256]{0:T(256)S(1)} %dynamic_slice.54) | copy-start | bytes 3076
  2731.7 6.4 copy-start.33
  (8 other events, 9.1 us)
Sparse Core Ops, SparseCore 0:
  9.9 241.9 all-gather.3
  253.8 161.5 all-gather.5
  417.3 160.7 all-gather.7
  610.3 384.5 reduce-scatter.2
  998.7 740.8 reduce-scatter.4
  1747.0 124.0 all-reduce.4
  1875.1 837.7 all-reduce.6
